TPU v7x, 256 devices: a whole 4x4x8 slice. The times are simulated.
256 devices in a mesh: view: 2 (over core), sky: 128 (over z, x, y).
Axes of the slice: x: 4, y: 4, z: 8, core: 2. Of those that a mesh axis runs over, the one named last changes fastest.
Arguments:
- pixels: bfloat16 [2, 262144, 128], P('view', 'sky'), may hold values from -6 to 6
- cotangent: bfloat16 [2, 262144, 128], P('view', 'sky'), may hold values from -6 to 6
- filters: bfloat16 [4, 128, 128], replicated, may hold values from -0.25 to 0.25
- lap_tiles: bfloat16 [128, 24, 256, 256], P('sky'), may hold values from -0.15625 to 0.15625
- tile_target: int32 [128, 24], P('sky'), may hold values from 0 to 7
- tile_source: int32 [128, 24], P('sky'), may hold values from 0 to 15
- tile_count: int32 [128], P('sky'), may hold values from 12 to 24, as said below
- send_blocks: int32 [128, 4, 2], P('sky'), may hold values from 0 to 7
Outputs:
- outputs: bfloat16 [2, 262144, 128], P('view', 'sky')
- pixel_grad: bfloat16 [2, 262144, 128], P('view', 'sky')
- filter_grad: float32 [4, 128, 128], replicated
Inputs may be any that keep to these rules, and one draw needn't show every extreme that they name: `tile_count`: every device has at least half of 24 live tiles, and some device has exactly 24. `tile_source`: indices below 8 are own blocks, the others received ones.
All inputs are finite; a program needn't handle non-finite values.
Results may differ from a plain program's by a relative error of at most 0.017.
Values may be sent and summed in bfloat16 or wider, within the bound.
No kernel may reach another device: no remote copies, remote signals or barrier semaphores. Data moves between devices by JAX's collectives and lax.ppermute only.
A program may use at most 64 MiB of HBM per device.

v0:
```python
import math
import jax
import jax.numpy as jnp
from jax import lax
from jax.sharding import PartitionSpec as P

OFFSETS = (1, -1, 2, -2)


def passed_along(array, axis, by):
    size = lax.axis_size(axis)
    pairs = [(i, i + by) for i in range(size) if 0 <= i + by < size]
    return lax.ppermute(array, axis, pairs)


def spread_forward(pieces):
    return [passed_along(portion, "sky", offset) for offset, portion in zip(OFFSETS, pieces)]


def spread_backward(pieces):
    return [passed_along(portion, "sky", -offset) for offset, portion in zip(OFFSETS, pieces)]


def tile_products(values, tile_set, target, source, live_count, out_count, transposed):
    contraction = "tpq,tpc->tqc" if transposed else "tpq,tqc->tpc"
    picked = values[target] if transposed else values[source]
    routed = source if transposed else target
    products = jnp.einsum(contraction, tile_set, picked, preferred_element_type=jnp.float32)
    live_mask = jnp.arange(routed.shape[0]) < live_count
    routing = ((routed[None, :] == jnp.arange(out_count)[:, None]) & live_mask[None, :]).astype(
        jnp.float32
    )
    return jnp.einsum("bt,tpc->bpc", routing, products)


def per_device(
    pixels, cotangent, filters, lap_tiles, tile_target, tile_source, tile_count, send_blocks
):
    block_size = lap_tiles.shape[2]
    channels = pixels.shape[2]
    row_count = pixels.shape[1]
    block_count = row_count // block_size
    send_count = send_blocks.shape[2]
    ext_count = block_count + 4 * send_count
    tile_set = lap_tiles[0]
    target = tile_target[0]
    source = tile_source[0]
    live_count = tile_count[0]
    chosen = send_blocks[0]

    def forward_pieces(blocks):
        return [blocks[chosen[number]] for number in range(4)]

    def forward_finish(blocks, arrived):
        extended = jnp.concatenate([blocks] + arrived, axis=0)
        return tile_products(extended, tile_set, target, source, live_count, block_count, False)

    def transposed_start(blocks):
        slot_sums = tile_products(blocks, tile_set, target, source, live_count, ext_count, True)
        pieces = [
            slot_sums[block_count + number * send_count : block_count + (number + 1) * send_count]
            for number in range(4)
        ]
        return (slot_sums, pieces)

    def transposed_finish(slot_sums, arrived):
        combined = slot_sums[:block_count]
        for number in range(4):
            routing = (chosen[number][None, :] == jnp.arange(block_count)[:, None]).astype(
                jnp.float32
            )
            combined = combined + jnp.einsum("bj,jqc->bqc", routing, arrived[number])
        return combined

    def apply_forward(blocks):
        return forward_finish(blocks, spread_forward(forward_pieces(blocks)))

    def apply_transposed(blocks):
        slot_sums, pieces = transposed_start(blocks)
        return transposed_finish(slot_sums, spread_backward(pieces))

    upstream = cotangent[0]

    def filter_term(member):
        return jnp.einsum("pc,pd->cd", member, upstream, preferred_element_type=jnp.float32)

    base = pixels[0].reshape(block_count, block_size, channels)
    pulled = [
        jnp.einsum(
            "pd,cd->pc", upstream, filters[order], preferred_element_type=jnp.float32
        ).reshape(block_count, block_size, channels)
        for order in range(4)
    ]
    adj_three = pulled[3]
    grad_terms = [filter_term(pixels[0])]
    cheb_one = apply_forward(base).astype(jnp.bfloat16)
    grad_terms.append(filter_term(cheb_one.reshape(row_count, channels)))
    cheb_two = (2.0 * apply_forward(cheb_one) - base.astype(jnp.float32)).astype(jnp.bfloat16)
    grad_terms.append(filter_term(cheb_two.reshape(row_count, channels)))
    cheb_three = (2.0 * apply_forward(cheb_two) - cheb_one.astype(jnp.float32)).astype(jnp.bfloat16)
    grad_terms.append(filter_term(cheb_three.reshape(row_count, channels)))
    adj_two = pulled[2] + 2.0 * apply_transposed(adj_three.astype(jnp.bfloat16))
    adj_one = pulled[1] + 2.0 * apply_transposed(adj_two.astype(jnp.bfloat16)) - adj_three
    adj_zero = pulled[0] + apply_transposed(adj_one.astype(jnp.bfloat16)) - adj_two
    flattened = [
        member.reshape(row_count, channels) for member in (base, cheb_one, cheb_two, cheb_three)
    ]
    result = jnp.dot(flattened[0], filters[0], preferred_element_type=jnp.float32)
    for order in range(1, 4):
        result = result + jnp.dot(
            flattened[order], filters[order], preferred_element_type=jnp.float32
        )
    outputs = result.astype(jnp.bfloat16).reshape(1, row_count, channels)
    pixel_grad = adj_zero.astype(jnp.bfloat16).reshape(1, row_count, channels)
    stacked = lax.psum(jnp.stack(grad_terms), ("view", "sky"))
    scale = 1.0 / math.sqrt(lax.axis_size("view") * lax.axis_size("sky") * row_count)
    return (outputs, pixel_grad, stacked * scale)


def solution(mesh):
    return jax.shard_map(
        per_device,
        mesh=mesh,
        in_specs=(
            P("view", "sky", None),
            P("view", "sky", None),
            P(),
            P("sky", None, None, None),
            P("sky", None),
            P("sky", None),
            P("sky"),
            P("sky", None, None),
        ),
        out_specs=(P("view", "sky", None), P("view", "sky", None), P()),
        check_vma=False,
    )
```

profile of v0, /device:TPU:2, one launch (start us, length us, event | category | flops | bytes accessed | tf_op | source)
XLA Modules:
  0.0 553.1 jit_solution(11454189926382703795)
XLA Ops:
  10.6 3.0 gather_fusion.15
  13.6 3.3 fusion.16
  16.9 2.8 copy.48
  24.6 5.1 collective-permute-start.15
  29.7 3.2 collective-permute-start.14
  32.9 3.5 collective-permute-start.13
  44.8 5.5 collective-permute-start.1
  67.9 6.3 %collective-permute-start.3 = (bf16[2,256,128]{2,1,0:T(8,128)(2,1)}, bf16[2,256,128]{2,1,0:T(8,128)(2,1)S(1)}, u32[]{:S(2)}, u32[]{:S(2)}) collective-permute-start(bf16[2,256,128]{2,1,0:T(8,128)(2,1)} %gather_fusion.3), channel_id=1, source_target_pairs={{2,0},{3,1},{4,2},{5,3},{6,4},{7,5},{8,6},{9,7},{10,8},{11,9},{12,... | collective-permute-start | bytes 393224 | tf_op jit(solution)/shard_map/ppermute | solution.py:13
  78.8 3.3 gather_fusion.4
  82.1 3.8 fusion.22
  85.8 2.8 copy.42
  107.8 3.1 gather_fusion.16
  111.0 3.2 fusion.14
  119.9 6.8 %collective-permute-start.19 = (bf16[2,256,128]{2,0,1:T(2,128)(2,1)}, bf16[2,256,128]{2,0,1:T(2,128)(2,1)}, u32[]{:S(2)}, u32[]{:S(2)}) collective-permute-start(bf16[2,256,128]{2,0,1:T(2,128)(2,1)} %get-tuple-element.12), channel_id=1, source_target_pairs={{0,2},{1,3},{2,4},{3,5},{4,6},{5,7},{6,8},{7,9},{8,10},{9,11},{10,... | collective-permute-start | bytes 393224 | tf_op jit(solution)/shard_map/ppermute | solution.py:13
  129.0 6.3 %collective-permute-start.5 = (bf16[2,256,128]{2,0,1:T(2,128)(2,1)S(1)}, bf16[2,256,128]{2,0,1:T(2,128)(2,1)}, u32[]{:S(2)}, u32[]{:S(2)}) collective-permute-start(bf16[2,256,128]{2,0,1:T(2,128)(2,1)S(1)} %copy.18), channel_id=1, source_target_pairs={{1,0},{2,1},{3,2},{4,3},{5,4},{6,5},{7,6},{8,7},{9,8},{10,9},{11,1... | collective-permute-start | bytes 393224 | tf_op jit(solution)/shard_map/ppermute | solution.py:13
  137.6 6.3 %collective-permute-start.7 = (bf16[2,256,128]{2,0,1:T(2,128)(2,1)S(1)}, bf16[2,256,128]{2,0,1:T(2,128)(2,1)S(1)}, u32[]{:S(2)}, u32[]{:S(2)}) collective-permute-start(bf16[2,256,128]{2,0,1:T(2,128)(2,1)S(1)} %copy.22), channel_id=1, source_target_pairs={{2,0},{3,1},{4,2},{5,3},{6,4},{7,5},{8,6},{9,7},{10,8},{11,9},{12,... | collective-permute-start | bytes 393224 | tf_op jit(solution)/shard_map/ppermute | solution.py:13
  150.1 6.0 %collective-permute-start.16 = (bf16[2,256,128]{2,0,1:T(2,128)(2,1)}, bf16[2,256,128]{2,0,1:T(2,128)(2,1)}, u32[]{:S(2)}, u32[]{:S(2)}) collective-permute-start(bf16[2,256,128]{2,0,1:T(2,128)(2,1)} %get-tuple-element.11), channel_id=1, source_target_pairs={{1,0},{2,1},{3,2},{4,3},{5,4},{6,5},{7,6},{8,7},{9,8},{10,9},{11,1... | collective-permute-start | bytes 393224 | tf_op jit(solution)/shard_map/ppermute | solution.py:13
  156.1 6.4 %concatenate.10 = bf16[16,256,128]{2,0,1:T(8,128)(2,1)} concatenate(bf16[8,256,128]{2,0,1:T(8,128)(2,1)} %copy-done.6, bf16[2,256,128]{2,0,1:T(2,128)(2,1)} %collective-permute-done.4, bf16[2,256,128]{2,0,1:T(2,128)(2,1)} %collective-permute-done.5, bf16[2,256,128]{2,0,1:T(2,128)(2,1)S(1)} %collective-permute-done.6, bf16[2,256,128]{2,0,1:T(2,128)(2,1)S(1)} %collective-permute-done.7), dimensions={0} | concatenate | bytes 2097152 | tf_op jit(solution)/shard_map/concatenate | solution.py:55
  165.0 3.3 gather_fusion.9
  168.3 3.8 fusion.20
  194.5 3.1 gather_fusion.17
  197.6 3.2 fusion.12
  207.9 2.8 collective-permute-start.21
  210.7 4.6 collective-permute-start.23
  215.3 5.4 collective-permute-start.20
  220.8 3.3 collective-permute-start.10
  226.4 5.1 collective-permute-start.11
  234.2 6.3 %collective-permute-start.9 = (bf16[2,256,128]{2,0,1:T(2,128)(2,1)S(1)}, bf16[2,256,128]{2,0,1:T(2,128)(2,1)}, u32[]{:S(2)}, u32[]{:S(2)}) collective-permute-start(bf16[2,256,128]{2,0,1:T(2,128)(2,1)S(1)} %copy.29), channel_id=1, source_target_pairs={{1,0},{2,1},{3,2},{4,3},{5,4},{6,5},{7,6},{8,7},{9,8},{10,9},{11,1... | collective-permute-start | bytes 393224 | tf_op jit(solution)/shard_map/ppermute | solution.py:13
  242.8 6.5 %concatenate.11 = bf16[16,256,128]{2,0,1:T(8,128)(2,1)} concatenate(bf16[8,256,128]{2,0,1:T(8,128)(2,1)} %copy-done.13, bf16[2,256,128]{2,0,1:T(2,128)(2,1)} %collective-permute-done.8, bf16[2,256,128]{2,0,1:T(2,128)(2,1)} %collective-permute-done.9, bf16[2,256,128]{2,0,1:T(2,128)(2,1)} %collective-permute-done.10, bf16[2,256,128]{2,0,1:T(2,128)(2,1)S(1)} %collective-permute-done.11), dimensions={0} | concatenate | bytes 2097152 | tf_op jit(solution)/shard_map/concatenate | solution.py:55
  251.7 3.3 gather_fusion.14
  255.0 3.7 fusion.18
  267.6 277.0 %all-reduce.2.cloned.1.call-done = f32[4,128,128]{2,1,0:T(8,128)} async-done(((f32[4,128,128]{2,1,0:T(8,128)}), f32[4,128,128]{2,1,0:T(8,128)}) %all-reduce.2.cloned.1.call-update) | async-done | bytes 262160 | tf_op jit(solution)/shard_map/psum | solution.py:115
  (197 shorter events, 125.6 us)
Async XLA Ops:
  7.2 537.4 %all-reduce.2.cloned.1.call-start = ((), (), s32[]{:S(2)}) async-start(), calls=%async_computation | async-start | bytes 524288 | tf_op jit(solution)/shard_map/psum | solution.py:115
  23.5 26.8 %copy-start.21 = (bf16[4,128,128]{2,1,0:T(8,128)(2,1)S(1)}, bf16[4,128,128]{2,1,0:T(8,128)(2,1)}, u32[]{:S(2)}) copy-start(bf16[4,128,128]{2,1,0:T(8,128)(2,1)} %param.10) | copy-start | bytes 393220
  24.6 75.7 %collective-permute-start.15 = (bf16[2,256,128]{2,0,1:T(2,128)(2,1)}, bf16[2,256,128]{2,0,1:T(2,128)(2,1)}, u32[]{:S(2)}, u32[]{:S(2)}) collective-permute-start(bf16[2,256,128]{2,0,1:T(2,128)(2,1)} %get-tuple-element.16), channel_id=1, source_target_pairs={{0,2},{1,3},{2,4},{3,5},{4,6},{5,7},{6,8},{7,9},{8,10},{9,11},{10,... | collective-permute-start | bytes 393224 | tf_op jit(solution)/shard_map/ppermute | solution.py:13
  29.7 72.1 %collective-permute-start.14 = (bf16[2,256,128]{2,0,1:T(2,128)(2,1)}, bf16[2,256,128]{2,0,1:T(2,128)(2,1)}, u32[]{:S(2)}, u32[]{:S(2)}) collective-permute-start(bf16[2,256,128]{2,0,1:T(2,128)(2,1)} %get-tuple-element.17), channel_id=1, source_target_pairs={{2,0},{3,1},{4,2},{5,3},{6,4},{7,5},{8,6},{9,7},{10,8},{11,9},{12,... | collective-permute-start | bytes 393224 | tf_op jit(solution)/shard_map/ppermute | solution.py:13
  32.9 70.3 %collective-permute-start.13 = (bf16[2,256,128]{2,0,1:T(2,128)(2,1)}, bf16[2,256,128]{2,0,1:T(2,128)(2,1)}, u32[]{:S(2)}, u32[]{:S(2)}) collective-permute-start(bf16[2,256,128]{2,0,1:T(2,128)(2,1)} %get-tuple-element.18), channel_id=1, source_target_pairs={{0,1},{1,2},{2,3},{3,4},{4,5},{5,6},{6,7},{7,8},{8,9},{9,10},{10,1... | collective-permute-start | bytes 393224 | tf_op jit(solution)/shard_map/ppermute | solution.py:13
  39.4 25.9 %collective-permute-start = (bf16[2,256,128]{2,1,0:T(8,128)(2,1)}, bf16[2,256,128]{2,1,0:T(8,128)(2,1)S(1)}, u32[]{:S(2)}, u32[]{:S(2)}) collective-permute-start(bf16[2,256,128]{2,1,0:T(8,128)(2,1)} %gather_fusion), channel_id=1, source_target_pairs={{0,1},{1,2},{2,3},{3,4},{4,5},{5,6},{6,7},{7,8},{8,9},{9,10},{10,1... | collective-permute-start | bytes 393224 | tf_op jit(solution)/shard_map/ppermute | solution.py:13
  44.8 23.0 %collective-permute-start.1 = (bf16[2,256,128]{2,1,0:T(8,128)(2,1)}, bf16[2,256,128]{2,1,0:T(8,128)(2,1)S(1)}, u32[]{:S(2)}, u32[]{:S(2)}) collective-permute-start(bf16[2,256,128]{2,1,0:T(8,128)(2,1)} %gather_fusion.1), channel_id=1, source_target_pairs={{1,0},{2,1},{3,2},{4,3},{5,4},{6,5},{7,6},{8,7},{9,8},{10,9},{11,1... | collective-permute-start | bytes 393224 | tf_op jit(solution)/shard_map/ppermute | solution.py:13
  65.3 9.6 %collective-permute-start.2 = (bf16[2,256,128]{2,1,0:T(8,128)(2,1)}, bf16[2,256,128]{2,1,0:T(8,128)(2,1)S(1)}, u32[]{:S(2)}, u32[]{:S(2)}) collective-permute-start(bf16[2,256,128]{2,1,0:T(8,128)(2,1)} %gather_fusion.2), channel_id=1, source_target_pairs={{0,2},{1,3},{2,4},{3,5},{4,6},{5,7},{6,8},{7,9},{8,10},{9,11},{10,... | collective-permute-start | bytes 393224 | tf_op jit(solution)/shard_map/ppermute | solution.py:13
  67.9 10.3 %collective-permute-start.3 = (bf16[2,256,128]{2,1,0:T(8,128)(2,1)}, bf16[2,256,128]{2,1,0:T(8,128)(2,1)S(1)}, u32[]{:S(2)}, u32[]{:S(2)}) collective-permute-start(bf16[2,256,128]{2,1,0:T(8,128)(2,1)} %gather_fusion.3), channel_id=1, source_target_pairs={{2,0},{3,1},{4,2},{5,3},{6,4},{7,5},{8,6},{9,7},{10,8},{11,9},{12,... | collective-permute-start | bytes 393224 | tf_op jit(solution)/shard_map/ppermute | solution.py:13
  74.8 29.6 %collective-permute-start.12 = (bf16[2,256,128]{2,0,1:T(2,128)(2,1)}, bf16[2,256,128]{2,0,1:T(2,128)(2,1)}, u32[]{:S(2)}, u32[]{:S(2)}) collective-permute-start(bf16[2,256,128]{2,0,1:T(2,128)(2,1)} %get-tuple-element.15), channel_id=1, source_target_pairs={{1,0},{2,1},{3,2},{4,3},{5,4},{6,5},{7,6},{8,7},{9,8},{10,9},{11,1... | collective-permute-start | bytes 393224 | tf_op jit(solution)/shard_map/ppermute | solution.py:13
  118.8 26.4 %copy-start.11 = (f32[16,256,128]{2,0,1:T(8,128)}, f32[16,256,128]{2,0,1:T(8,128)S(1)}, u32[]{:S(2)}) copy-start(f32[16,256,128]{2,0,1:T(8,128)S(1)} %fusion.2) | copy-start | bytes 6291460
  118.8 25.1 %copy-start.8 = (bf16[8,256,128]{2,1,0:T(8,128)(2,1)S(1)}, bf16[8,256,128]{2,1,0:T(8,128)(2,1)}, u32[]{:S(2)}) copy-start(bf16[8,256,128]{2,1,0:T(8,128)(2,1)} %copy.14) | copy-start | bytes 1572868
  118.8 25.1 %copy-start.17 = (f32[2048,128]{1,0:T(8,128)S(1)}, f32[2048,128]{1,0:T(8,128)}, u32[]{:S(2)}) copy-start(f32[2048,128]{1,0:T(8,128)} %fusion.70) | copy-start | bytes 3145732
  119.9 67.0 %collective-permute-start.19 = (bf16[2,256,128]{2,0,1:T(2,128)(2,1)}, bf16[2,256,128]{2,0,1:T(2,128)(2,1)}, u32[]{:S(2)}, u32[]{:S(2)}) collective-permute-start(bf16[2,256,128]{2,0,1:T(2,128)(2,1)} %get-tuple-element.12), channel_id=1, source_target_pairs={{0,2},{1,3},{2,4},{3,5},{4,6},{5,7},{6,8},{7,9},{8,10},{9,11},{10,... | collective-permute-start | bytes 393224 | tf_op jit(solution)/shard_map/ppermute | solution.py:13
  126.9 19.2 %collective-permute-start.4 = (bf16[2,256,128]{2,0,1:T(2,128)(2,1)S(1)}, bf16[2,256,128]{2,0,1:T(2,128)(2,1)}, u32[]{:S(2)}, u32[]{:S(2)}) collective-permute-start(bf16[2,256,128]{2,0,1:T(2,128)(2,1)S(1)} %copy.16), channel_id=1, source_target_pairs={{0,1},{1,2},{2,3},{3,4},{4,5},{5,6},{6,7},{7,8},{8,9},{9,10},{10,1... | collective-permute-start | bytes 393224 | tf_op jit(solution)/shard_map/ppermute | solution.py:13
  129.0 19.1 %collective-permute-start.5 = (bf16[2,256,128]{2,0,1:T(2,128)(2,1)S(1)}, bf16[2,256,128]{2,0,1:T(2,128)(2,1)}, u32[]{:S(2)}, u32[]{:S(2)}) collective-permute-start(bf16[2,256,128]{2,0,1:T(2,128)(2,1)S(1)} %copy.18), channel_id=1, source_target_pairs={{1,0},{2,1},{3,2},{4,3},{5,4},{6,5},{7,6},{8,7},{9,8},{10,9},{11,1... | collective-permute-start | bytes 393224 | tf_op jit(solution)/shard_map/ppermute | solution.py:13
  135.5 14.5 %collective-permute-start.6 = (bf16[2,256,128]{2,0,1:T(2,128)(2,1)S(1)}, bf16[2,256,128]{2,0,1:T(2,128)(2,1)S(1)}, u32[]{:S(2)}, u32[]{:S(2)}) collective-permute-start(bf16[2,256,128]{2,0,1:T(2,128)(2,1)S(1)} %copy.20), channel_id=1, source_target_pairs={{0,2},{1,3},{2,4},{3,5},{4,6},{5,7},{6,8},{7,9},{8,10},{9,11},{10,... | collective-permute-start | bytes 393224 | tf_op jit(solution)/shard_map/ppermute | solution.py:13
  137.6 18.5 %collective-permute-start.7 = (bf16[2,256,128]{2,0,1:T(2,128)(2,1)S(1)}, bf16[2,256,128]{2,0,1:T(2,128)(2,1)S(1)}, u32[]{:S(2)}, u32[]{:S(2)}) collective-permute-start(bf16[2,256,128]{2,0,1:T(2,128)(2,1)S(1)} %copy.22), channel_id=1, source_target_pairs={{2,0},{3,1},{4,2},{5,3},{6,4},{7,5},{8,6},{9,7},{10,8},{11,9},{12,... | collective-permute-start | bytes 393224 | tf_op jit(solution)/shard_map/ppermute | solution.py:13
  146.2 42.2 %collective-permute-start.18 = (bf16[2,256,128]{2,0,1:T(2,128)(2,1)}, bf16[2,256,128]{2,0,1:T(2,128)(2,1)}, u32[]{:S(2)}, u32[]{:S(2)}) collective-permute-start(bf16[2,256,128]{2,0,1:T(2,128)(2,1)} %get-tuple-element.13), channel_id=1, source_target_pairs={{2,0},{3,1},{4,2},{5,3},{6,4},{7,5},{8,6},{9,7},{10,8},{11,9},{12,... | collective-permute-start | bytes 393224 | tf_op jit(solution)/shard_map/ppermute | solution.py:13
  148.1 41.6 %collective-permute-start.17 = (bf16[2,256,128]{2,0,1:T(2,128)(2,1)}, bf16[2,256,128]{2,0,1:T(2,128)(2,1)}, u32[]{:S(2)}, u32[]{:S(2)}) collective-permute-start(bf16[2,256,128]{2,0,1:T(2,128)(2,1)} %get-tuple-element.14), channel_id=1, source_target_pairs={{0,1},{1,2},{2,3},{3,4},{4,5},{5,6},{6,7},{7,8},{8,9},{9,10},{10,1... | collective-permute-start | bytes 393224 | tf_op jit(solution)/shard_map/ppermute | solution.py:13
  150.1 41.0 %collective-permute-start.16 = (bf16[2,256,128]{2,0,1:T(2,128)(2,1)}, bf16[2,256,128]{2,0,1:T(2,128)(2,1)}, u32[]{:S(2)}, u32[]{:S(2)}) collective-permute-start(bf16[2,256,128]{2,0,1:T(2,128)(2,1)} %get-tuple-element.11), channel_id=1, source_target_pairs={{1,0},{2,1},{3,2},{4,3},{5,4},{6,5},{7,6},{8,7},{9,8},{10,9},{11,1... | collective-permute-start | bytes 393224 | tf_op jit(solution)/shard_map/ppermute | solution.py:13
  205.4 19.0 %copy-start.22 = (bf16[2,256,128]{2,1,0:T(8,128)(2,1)S(1)}, bf16[2,256,128]{2,1,0:T(8,128)(2,1)}, u32[]{:S(2)}) copy-start(bf16[2,256,128]{2,1,0:T(8,128)(2,1)} %gather_fusion.11) | copy-start | bytes 393220
  205.5 19.2 %copy-start.7 = (bf16[8,256,128]{2,1,0:T(8,128)(2,1)S(1)}, bf16[8,256,128]{2,1,0:T(8,128)(2,1)}, u32[]{:S(2)}) copy-start(bf16[8,256,128]{2,1,0:T(8,128)(2,1)} %copy.25) | copy-start | bytes 1572868
  205.5 19.2 %copy-start.20 = (f32[2048,128]{1,0:T(8,128)S(1)}, f32[2048,128]{1,0:T(8,128)}, u32[]{:S(2)}) copy-start(f32[2048,128]{1,0:T(8,128)} %convolution_add_fusion.2) | copy-start | bytes 3145732
  205.8 20.5 %collective-permute-start.22 = (bf16[2,256,128]{2,0,1:T(2,128)(2,1)S(1)}, bf16[2,256,128]{2,0,1:T(2,128)(2,1)S(1)}, u32[]{:S(2)}, u32[]{:S(2)}) collective-permute-start(bf16[2,256,128]{2,0,1:T(2,128)(2,1)S(1)} %get-tuple-element.9), channel_id=1, source_target_pairs={{2,0},{3,1},{4,2},{5,3},{6,4},{7,5},{8,6},{9,7},{10,8},{11,9},{12,... | collective-permute-start | bytes 393224 | tf_op jit(solution)/shard_map/ppermute | solution.py:13
  207.9 24.0 %collective-permute-start.21 = (bf16[2,256,128]{2,0,1:T(2,128)(2,1)S(1)}, bf16[2,256,128]{2,0,1:T(2,128)(2,1)S(1)}, u32[]{:S(2)}, u32[]{:S(2)}) collective-permute-start(bf16[2,256,128]{2,0,1:T(2,128)(2,1)S(1)} %get-tuple-element.10), channel_id=1, source_target_pairs={{0,1},{1,2},{2,3},{3,4},{4,5},{5,6},{6,7},{7,8},{8,9},{9,10},{10,1... | collective-permute-start | bytes 393224 | tf_op jit(solution)/shard_map/ppermute | solution.py:13
  210.7 23.5 %collective-permute-start.23 = (bf16[2,256,128]{2,0,1:T(2,128)(2,1)S(1)}, bf16[2,256,128]{2,0,1:T(2,128)(2,1)S(1)}, u32[]{:S(2)}, u32[]{:S(2)}) collective-permute-start(bf16[2,256,128]{2,0,1:T(2,128)(2,1)S(1)} %get-tuple-element.8), channel_id=1, source_target_pairs={{0,2},{1,3},{2,4},{3,5},{4,6},{5,7},{6,8},{7,9},{8,10},{9,11},{10,... | collective-permute-start | bytes 393224 | tf_op jit(solution)/shard_map/ppermute | solution.py:13
  215.3 25.6 %collective-permute-start.20 = (bf16[2,256,128]{2,0,1:T(2,128)(2,1)S(1)}, bf16[2,256,128]{2,0,1:T(2,128)(2,1)S(1)}, u32[]{:S(2)}, u32[]{:S(2)}) collective-permute-start(bf16[2,256,128]{2,0,1:T(2,128)(2,1)S(1)} %get-tuple-element.7), channel_id=1, source_target_pairs={{1,0},{2,1},{3,2},{4,3},{5,4},{6,5},{7,6},{8,7},{9,8},{10,9},{11,1... | collective-permute-start | bytes 393224 | tf_op jit(solution)/shard_map/ppermute | solution.py:13
  220.8 21.7 %collective-permute-start.10 = (bf16[2,256,128]{2,0,1:T(2,128)(2,1)S(1)}, bf16[2,256,128]{2,0,1:T(2,128)(2,1)}, u32[]{:S(2)}, u32[]{:S(2)}) collective-permute-start(bf16[2,256,128]{2,0,1:T(2,128)(2,1)S(1)} %copy.31), channel_id=1, source_target_pairs={{0,2},{1,3},{2,4},{3,5},{4,6},{5,7},{6,8},{7,9},{8,10},{9,11},{10,... | collective-permute-start | bytes 393224 | tf_op jit(solution)/shard_map/ppermute | solution.py:13
  226.4 16.2 %collective-permute-start.11 = (bf16[2,256,128]{2,0,1:T(2,128)(2,1)S(1)}, bf16[2,256,128]{2,0,1:T(2,128)(2,1)S(1)}, u32[]{:S(2)}, u32[]{:S(2)}) collective-permute-start(bf16[2,256,128]{2,0,1:T(2,128)(2,1)S(1)} %copy.33), channel_id=1, source_target_pairs={{2,0},{3,1},{4,2},{5,3},{6,4},{7,5},{8,6},{9,7},{10,8},{11,9},{12,... | collective-permute-start | bytes 393224 | tf_op jit(solution)/shard_map/ppermute | solution.py:13
  231.9 10.7 %collective-permute-start.8 = (bf16[2,256,128]{2,0,1:T(2,128)(2,1)S(1)}, bf16[2,256,128]{2,0,1:T(2,128)(2,1)}, u32[]{:S(2)}, u32[]{:S(2)}) collective-permute-start(bf16[2,256,128]{2,0,1:T(2,128)(2,1)S(1)} %copy.27), channel_id=1, source_target_pairs={{0,1},{1,2},{2,3},{3,4},{4,5},{5,6},{6,7},{7,8},{8,9},{9,10},{10,1... | collective-permute-start | bytes 393224 | tf_op jit(solution)/shard_map/ppermute | solution.py:13
  234.2 8.5 %collective-permute-start.9 = (bf16[2,256,128]{2,0,1:T(2,128)(2,1)S(1)}, bf16[2,256,128]{2,0,1:T(2,128)(2,1)}, u32[]{:S(2)}, u32[]{:S(2)}) collective-permute-start(bf16[2,256,128]{2,0,1:T(2,128)(2,1)S(1)} %copy.29), channel_id=1, source_target_pairs={{1,0},{2,1},{3,2},{4,3},{5,4},{6,5},{7,6},{8,7},{9,8},{10,9},{11,1... | collective-permute-start | bytes 393224 | tf_op jit(solution)/shard_map/ppermute | solution.py:13
  (32 other events, 177.5 us)
Sparse Core Ops, SparseCore 0:
  265.3 279.2 all-reduce.1
where the time goes:
time: 556 us; the launch traced here: 553 us
  waiting for transfers between devices  278 us (50%)
  local copies, waits for them, and re-layouts  95.7 us (17%)
  starting transfers between devices  94.5 us (17%)
  matrix products  64.3 us (12%)
  between operations  15.6 us (3%)
    psum x1, waiting for transfers between devices, per_device(): stacked = lax.psum(jnp.stack(grad_terms), ('view', 'sky'))  277 us
    ppermute x24, starting transfers between devices, passed_along(): return lax.ppermute(array, axis, pairs)  94.5 us
    gather x20, local copies, waits for them, and re-layouts, forward_pieces(): return [blocks[chosen[number]] for number in range(4)]  26.8 us
    dot_general x6, matrix products, tile_products(): jnp.einsum(contraction, tile_set, picked, preferred_element_type=jnp.floa...  20.9 us
    gather x6, local copies, waits for them, and re-layouts, tile_products(): picked = values[target] if transposed else values[source]  19.1 us
    concatenate x5, local copies, waits for them, and re-layouts, forward_finish(): extended = jnp.concatenate([blocks] + arrived, axis=0)  18.5 us
    dot_general x6, local copies, waits for them, and re-layouts, tile_products(): jnp.einsum(contraction, tile_set, picked, preferred_element_type=jnp.floa...  16.5 us
    dot_general x12, matrix products, transposed_finish(): combined = combined + jnp.einsum('bj,jqc->bqc', routing, arrived[number])  15 us
  transfers between devices with their start and end apart: 25, of which 3 were waited for; matrix products, arithmetic and copies ran while one was open for 17% of the time, Pallas kernels for 0%

commit v1 on v0

--- a/solution.py
+++ b/solution.py
@@ -112,7 +112,7 @@
         )
     outputs = result.astype(jnp.bfloat16).reshape(1, row_count, channels)
     pixel_grad = adj_zero.astype(jnp.bfloat16).reshape(1, row_count, channels)
-    stacked = lax.psum(jnp.stack(grad_terms), ("view", "sky"))
+    stacked = lax.psum(lax.psum(jnp.stack(grad_terms), "view"), "sky")
     scale = 1.0 / math.sqrt(lax.axis_size("view") * lax.axis_size("sky") * row_count)
     return (outputs, pixel_grad, stacked * scale)
 

time: 556 us -> 546 us (0.982)
  waiting for transfers between devices: 278 us -> 261 us
  matrix products: 64.3 us -> 71.4 us
    psum x1 -> x2, waiting for transfers between devices: 277 us -> 261 us  [per_device(): stacked = lax.psum(lax.psum(jnp.stack(grad_terms), 'view'), 'sky')]
    dot_general x12, matrix products: 15 us -> 23.5 us  [transposed_finish(): combined = combined + jnp.einsum('bj,jqc->bqc', routing, arrived[number])]
  transfers between devices with their start and end apart: 25 -> 26, of which waited for: 3 -> 3; matrix products, arithmetic and copies ran while one was open for 17% -> 22% of each run, Pallas kernels for 0% -> 0%
where the time goes in v1:
time: 546 us; the launch traced here: 542 us
  waiting for transfers between devices  261 us (48%)
  local copies, waits for them, and re-layouts  97.2 us (18%)
  starting transfers between devices  91.7 us (17%)
  matrix products  71.4 us (13%)
  between operations  15.7 us (3%)
    psum x2, waiting for transfers between devices, per_device(): stacked = lax.psum(lax.psum(jnp.stack(grad_terms), 'view'), 'sky')  261 us
    ppermute x24, starting transfers between devices, passed_along(): return lax.ppermute(array, axis, pairs)  91.6 us
    gather x20, local copies, waits for them, and re-layouts, forward_pieces(): return [blocks[chosen[number]] for number in range(4)]  26.8 us
    dot_general x12, matrix products, transposed_finish(): combined = combined + jnp.einsum('bj,jqc->bqc', routing, arrived[number])  23.5 us
    dot_general x6, matrix products, tile_products(): jnp.einsum(contraction, tile_set, picked, preferred_element_type=jnp.floa...  21 us
    gather x6, local copies, waits for them, and re-layouts, tile_products(): picked = values[target] if transposed else values[source]  19.1 us
    concatenate x5, local copies, waits for them, and re-layouts, forward_finish(): extended = jnp.concatenate([blocks] + arrived, axis=0)  18.7 us
    dot_general x6, local copies, waits for them, and re-layouts, tile_products(): jnp.einsum(contraction, tile_set, picked, preferred_element_type=jnp.floa...  16.6 us
  transfers between devices with their start and end apart: 26, of which 3 were waited for; matrix products, arithmetic and copies ran while one was open for 22% of the time, Pallas kernels for 0%

profile of v1, /device:TPU:2, one launch (start us, length us, event | category | flops | bytes accessed | tf_op | source)
XLA Modules:
  0.0 542.4 jit_solution(11402797703340161463)
XLA Ops:
  10.6 3.0 gather_fusion.15
  13.6 3.3 fusion.16
  16.9 2.8 copy.48
  24.7 5.1 collective-permute-start.15
  29.8 3.2 collective-permute-start.14
  32.9 3.5 collective-permute-start.13
  44.8 5.5 %collective-permute-start.1 = (bf16[2,256,128]{2,1,0:T(8,128)(2,1)}, bf16[2,256,128]{2,1,0:T(8,128)(2,1)S(1)}, u32[]{:S(2)}, u32[]{:S(2)}) collective-permute-start(bf16[2,256,128]{2,1,0:T(8,128)(2,1)} %gather_fusion.1), channel_id=1, source_target_pairs={{1,0},{2,1},{3,2},{4,3},{5,4},{6,5},{7,6},{8,7},{9,8},{10,9},{11,1... | collective-permute-start | bytes 393224 | tf_op jit(solution)/shard_map/ppermute | solution.py:13
  67.9 6.3 %collective-permute-start.3 = (bf16[2,256,128]{2,1,0:T(8,128)(2,1)}, bf16[2,256,128]{2,1,0:T(8,128)(2,1)S(1)}, u32[]{:S(2)}, u32[]{:S(2)}) collective-permute-start(bf16[2,256,128]{2,1,0:T(8,128)(2,1)} %gather_fusion.3), channel_id=1, source_target_pairs={{2,0},{3,1},{4,2},{5,3},{6,4},{7,5},{8,6},{9,7},{10,8},{11,9},{12,... | collective-permute-start | bytes 393224 | tf_op jit(solution)/shard_map/ppermute | solution.py:13
  78.8 3.3 gather_fusion.4
  82.1 3.8 fusion.22
  108.0 3.1 gather_fusion.16
  111.1 3.2 fusion.14
  120.1 6.8 %collective-permute-start.19 = (bf16[2,256,128]{2,0,1:T(2,128)(2,1)}, bf16[2,256,128]{2,0,1:T(2,128)(2,1)}, u32[]{:S(2)}, u32[]{:S(2)}) collective-permute-start(bf16[2,256,128]{2,0,1:T(2,128)(2,1)} %get-tuple-element.12), channel_id=1, source_target_pairs={{0,2},{1,3},{2,4},{3,5},{4,6},{5,7},{6,8},{7,9},{8,10},{9,11},{10,... | collective-permute-start | bytes 393224 | tf_op jit(solution)/shard_map/ppermute | solution.py:13
  129.2 6.3 %collective-permute-start.5 = (bf16[2,256,128]{2,0,1:T(2,128)(2,1)S(1)}, bf16[2,256,128]{2,0,1:T(2,128)(2,1)}, u32[]{:S(2)}, u32[]{:S(2)}) collective-permute-start(bf16[2,256,128]{2,0,1:T(2,128)(2,1)S(1)} %copy.18), channel_id=1, source_target_pairs={{1,0},{2,1},{3,2},{4,3},{5,4},{6,5},{7,6},{8,7},{9,8},{10,9},{11,1... | collective-permute-start | bytes 393224 | tf_op jit(solution)/shard_map/ppermute | solution.py:13
  137.8 6.3 %collective-permute-start.7 = (bf16[2,256,128]{2,0,1:T(2,128)(2,1)S(1)}, bf16[2,256,128]{2,0,1:T(2,128)(2,1)S(1)}, u32[]{:S(2)}, u32[]{:S(2)}) collective-permute-start(bf16[2,256,128]{2,0,1:T(2,128)(2,1)S(1)} %copy.22), channel_id=1, source_target_pairs={{2,0},{3,1},{4,2},{5,3},{6,4},{7,5},{8,6},{9,7},{10,8},{11,9},{12,... | collective-permute-start | bytes 393224 | tf_op jit(solution)/shard_map/ppermute | solution.py:13
  150.3 6.0 %collective-permute-start.16 = (bf16[2,256,128]{2,0,1:T(2,128)(2,1)}, bf16[2,256,128]{2,0,1:T(2,128)(2,1)}, u32[]{:S(2)}, u32[]{:S(2)}) collective-permute-start(bf16[2,256,128]{2,0,1:T(2,128)(2,1)} %get-tuple-element.11), channel_id=1, source_target_pairs={{1,0},{2,1},{3,2},{4,3},{5,4},{6,5},{7,6},{8,7},{9,8},{10,9},{11,1... | collective-permute-start | bytes 393224 | tf_op jit(solution)/shard_map/ppermute | solution.py:13
  156.3 6.5 %concatenate.10 = bf16[16,256,128]{2,0,1:T(8,128)(2,1)} concatenate(bf16[8,256,128]{2,0,1:T(8,128)(2,1)} %copy-done.6, bf16[2,256,128]{2,0,1:T(2,128)(2,1)} %collective-permute-done.4, bf16[2,256,128]{2,0,1:T(2,128)(2,1)} %collective-permute-done.5, bf16[2,256,128]{2,0,1:T(2,128)(2,1)S(1)} %collective-permute-done.6, bf16[2,256,128]{2,0,1:T(2,128)(2,1)S(1)} %collective-permute-done.7), dimensions={0} | concatenate | bytes 2097152 | tf_op jit(solution)/shard_map/concatenate | solution.py:55
  165.3 3.3 gather_fusion.9
  168.6 3.8 fusion.20
  194.7 3.1 gather_fusion.17
  197.9 3.2 fusion.12
  209.1 5.4 %collective-permute-start.10 = (bf16[2,256,128]{2,0,1:T(2,128)(2,1)S(1)}, bf16[2,256,128]{2,0,1:T(2,128)(2,1)S(1)}, u32[]{:S(2)}, u32[]{:S(2)}) collective-permute-start(bf16[2,256,128]{2,0,1:T(2,128)(2,1)S(1)} %copy.31), channel_id=1, source_target_pairs={{0,2},{1,3},{2,4},{3,5},{4,6},{5,7},{6,8},{7,9},{8,10},{9,11},{10,... | collective-permute-start | bytes 393224 | tf_op jit(solution)/shard_map/ppermute | solution.py:13
  214.7 3.0 collective-permute-start.11
  220.7 5.2 collective-permute-start.9
  229.5 4.8 collective-permute-start.23
  234.3 3.4 collective-permute-start.20
  237.8 6.5 %concatenate.11 = bf16[16,256,128]{2,0,1:T(8,128)(2,1)} concatenate(bf16[8,256,128]{2,0,1:T(8,128)(2,1)} %copy-done.14, bf16[2,256,128]{2,0,1:T(2,128)(2,1)} %copy-done.31, bf16[2,256,128]{2,0,1:T(2,128)(2,1)} %collective-permute-done.9, bf16[2,256,128]{2,0,1:T(2,128)(2,1)} %copy-done.29, bf16[2,256,128]{2,0,1:T(2,128)(2,1)} %copy-done.30), dimensions={0} | concatenate | bytes 2097152 | tf_op jit(solution)/shard_map/concatenate | solution.py:55
  246.8 3.3 gather_fusion.14
  250.1 3.8 fusion.18
  267.3 46.2 %all-reduce.3.cloned.1.call-done = f32[4,128,128]{2,1,0:T(8,128)} async-done(((f32[4,128,128]{2,1,0:T(8,128)}), f32[4,128,128]{2,1,0:T(8,128)}) %all-reduce.3.cloned.1.call-update) | async-done | bytes 262160 | tf_op jit(solution)/shard_map/psum | solution.py:115
  313.5 3.4 fusion.60
  319.4 214.5 %all-reduce.5.cloned.1.call-done = f32[4,128,128]{2,1,0:T(8,128)} async-done(((f32[4,128,128]{2,1,0:T(8,128)}), f32[4,128,128]{2,1,0:T(8,128)}) %all-reduce.5.cloned.1.call-update) | async-done | bytes 262160 | tf_op jit(solution)/shard_map/psum | solution.py:115
  (208 shorter events, 135.9 us)
Async XLA Ops:
  7.2 306.3 %all-reduce.3.cloned.1.call-start = ((), (), s32[]{:S(2)}) async-start(), calls=%async_computation | async-start | bytes 524288 | tf_op jit(solution)/shard_map/psum | solution.py:115
  23.5 26.8 %copy-start.22 = (bf16[4,128,128]{2,1,0:T(8,128)(2,1)S(1)}, bf16[4,128,128]{2,1,0:T(8,128)(2,1)}, u32[]{:S(2)}) copy-start(bf16[4,128,128]{2,1,0:T(8,128)(2,1)} %param.10) | copy-start | bytes 393220
  24.7 75.7 %collective-permute-start.15 = (bf16[2,256,128]{2,0,1:T(2,128)(2,1)}, bf16[2,256,128]{2,0,1:T(2,128)(2,1)}, u32[]{:S(2)}, u32[]{:S(2)}) collective-permute-start(bf16[2,256,128]{2,0,1:T(2,128)(2,1)} %get-tuple-element.16), channel_id=1, source_target_pairs={{0,2},{1,3},{2,4},{3,5},{4,6},{5,7},{6,8},{7,9},{8,10},{9,11},{10,... | collective-permute-start | bytes 393224 | tf_op jit(solution)/shard_map/ppermute | solution.py:13
  29.8 72.1 %collective-permute-start.14 = (bf16[2,256,128]{2,0,1:T(2,128)(2,1)}, bf16[2,256,128]{2,0,1:T(2,128)(2,1)}, u32[]{:S(2)}, u32[]{:S(2)}) collective-permute-start(bf16[2,256,128]{2,0,1:T(2,128)(2,1)} %get-tuple-element.17), channel_id=1, source_target_pairs={{2,0},{3,1},{4,2},{5,3},{6,4},{7,5},{8,6},{9,7},{10,8},{11,9},{12,... | collective-permute-start | bytes 393224 | tf_op jit(solution)/shard_map/ppermute | solution.py:13
  32.9 70.3 %collective-permute-start.13 = (bf16[2,256,128]{2,0,1:T(2,128)(2,1)}, bf16[2,256,128]{2,0,1:T(2,128)(2,1)}, u32[]{:S(2)}, u32[]{:S(2)}) collective-permute-start(bf16[2,256,128]{2,0,1:T(2,128)(2,1)} %get-tuple-element.18), channel_id=1, source_target_pairs={{0,1},{1,2},{2,3},{3,4},{4,5},{5,6},{6,7},{7,8},{8,9},{9,10},{10,1... | collective-permute-start | bytes 393224 | tf_op jit(solution)/shard_map/ppermute | solution.py:13
  39.4 25.9 %collective-permute-start = (bf16[2,256,128]{2,1,0:T(8,128)(2,1)}, bf16[2,256,128]{2,1,0:T(8,128)(2,1)S(1)}, u32[]{:S(2)}, u32[]{:S(2)}) collective-permute-start(bf16[2,256,128]{2,1,0:T(8,128)(2,1)} %gather_fusion), channel_id=1, source_target_pairs={{0,1},{1,2},{2,3},{3,4},{4,5},{5,6},{6,7},{7,8},{8,9},{9,10},{10,1... | collective-permute-start | bytes 393224 | tf_op jit(solution)/shard_map/ppermute | solution.py:13
  44.8 23.0 %collective-permute-start.1 = (bf16[2,256,128]{2,1,0:T(8,128)(2,1)}, bf16[2,256,128]{2,1,0:T(8,128)(2,1)S(1)}, u32[]{:S(2)}, u32[]{:S(2)}) collective-permute-start(bf16[2,256,128]{2,1,0:T(8,128)(2,1)} %gather_fusion.1), channel_id=1, source_target_pairs={{1,0},{2,1},{3,2},{4,3},{5,4},{6,5},{7,6},{8,7},{9,8},{10,9},{11,1... | collective-permute-start | bytes 393224 | tf_op jit(solution)/shard_map/ppermute | solution.py:13
  65.3 9.6 %collective-permute-start.2 = (bf16[2,256,128]{2,1,0:T(8,128)(2,1)}, bf16[2,256,128]{2,1,0:T(8,128)(2,1)S(1)}, u32[]{:S(2)}, u32[]{:S(2)}) collective-permute-start(bf16[2,256,128]{2,1,0:T(8,128)(2,1)} %gather_fusion.2), channel_id=1, source_target_pairs={{0,2},{1,3},{2,4},{3,5},{4,6},{5,7},{6,8},{7,9},{8,10},{9,11},{10,... | collective-permute-start | bytes 393224 | tf_op jit(solution)/shard_map/ppermute | solution.py:13
  67.9 10.3 %collective-permute-start.3 = (bf16[2,256,128]{2,1,0:T(8,128)(2,1)}, bf16[2,256,128]{2,1,0:T(8,128)(2,1)S(1)}, u32[]{:S(2)}, u32[]{:S(2)}) collective-permute-start(bf16[2,256,128]{2,1,0:T(8,128)(2,1)} %gather_fusion.3), channel_id=1, source_target_pairs={{2,0},{3,1},{4,2},{5,3},{6,4},{7,5},{8,6},{9,7},{10,8},{11,9},{12,... | collective-permute-start | bytes 393224 | tf_op jit(solution)/shard_map/ppermute | solution.py:13
  74.9 29.6 %collective-permute-start.12 = (bf16[2,256,128]{2,0,1:T(2,128)(2,1)}, bf16[2,256,128]{2,0,1:T(2,128)(2,1)}, u32[]{:S(2)}, u32[]{:S(2)}) collective-permute-start(bf16[2,256,128]{2,0,1:T(2,128)(2,1)} %get-tuple-element.15), channel_id=1, source_target_pairs={{1,0},{2,1},{3,2},{4,3},{5,4},{6,5},{7,6},{8,7},{9,8},{10,9},{11,1... | collective-permute-start | bytes 393224 | tf_op jit(solution)/shard_map/ppermute | solution.py:13
  119.0 26.4 %copy-start.12 = (f32[16,256,128]{2,0,1:T(8,128)}, f32[16,256,128]{2,0,1:T(8,128)S(1)}, u32[]{:S(2)}) copy-start(f32[16,256,128]{2,0,1:T(8,128)S(1)} %fusion.2) | copy-start | bytes 6291460
  119.0 25.1 %copy-start.8 = (bf16[8,256,128]{2,1,0:T(8,128)(2,1)S(1)}, bf16[8,256,128]{2,1,0:T(8,128)(2,1)}, u32[]{:S(2)}) copy-start(bf16[8,256,128]{2,1,0:T(8,128)(2,1)} %copy.14) | copy-start | bytes 1572868
  119.0 25.1 %copy-start.18 = (f32[2048,128]{1,0:T(8,128)S(1)}, f32[2048,128]{1,0:T(8,128)}, u32[]{:S(2)}) copy-start(f32[2048,128]{1,0:T(8,128)} %fusion.70) | copy-start | bytes 3145732
  120.1 67.1 %collective-permute-start.19 = (bf16[2,256,128]{2,0,1:T(2,128)(2,1)}, bf16[2,256,128]{2,0,1:T(2,128)(2,1)}, u32[]{:S(2)}, u32[]{:S(2)}) collective-permute-start(bf16[2,256,128]{2,0,1:T(2,128)(2,1)} %get-tuple-element.12), channel_id=1, source_target_pairs={{0,2},{1,3},{2,4},{3,5},{4,6},{5,7},{6,8},{7,9},{8,10},{9,11},{10,... | collective-permute-start | bytes 393224 | tf_op jit(solution)/shard_map/ppermute | solution.py:13
  127.1 19.3 %collective-permute-start.4 = (bf16[2,256,128]{2,0,1:T(2,128)(2,1)S(1)}, bf16[2,256,128]{2,0,1:T(2,128)(2,1)}, u32[]{:S(2)}, u32[]{:S(2)}) collective-permute-start(bf16[2,256,128]{2,0,1:T(2,128)(2,1)S(1)} %copy.16), channel_id=1, source_target_pairs={{0,1},{1,2},{2,3},{3,4},{4,5},{5,6},{6,7},{7,8},{8,9},{9,10},{10,1... | collective-permute-start | bytes 393224 | tf_op jit(solution)/shard_map/ppermute | solution.py:13
  129.2 19.1 %collective-permute-start.5 = (bf16[2,256,128]{2,0,1:T(2,128)(2,1)S(1)}, bf16[2,256,128]{2,0,1:T(2,128)(2,1)}, u32[]{:S(2)}, u32[]{:S(2)}) collective-permute-start(bf16[2,256,128]{2,0,1:T(2,128)(2,1)S(1)} %copy.18), channel_id=1, source_target_pairs={{1,0},{2,1},{3,2},{4,3},{5,4},{6,5},{7,6},{8,7},{9,8},{10,9},{11,1... | collective-permute-start | bytes 393224 | tf_op jit(solution)/shard_map/ppermute | solution.py:13
  135.7 14.5 %collective-permute-start.6 = (bf16[2,256,128]{2,0,1:T(2,128)(2,1)S(1)}, bf16[2,256,128]{2,0,1:T(2,128)(2,1)S(1)}, u32[]{:S(2)}, u32[]{:S(2)}) collective-permute-start(bf16[2,256,128]{2,0,1:T(2,128)(2,1)S(1)} %copy.20), channel_id=1, source_target_pairs={{0,2},{1,3},{2,4},{3,5},{4,6},{5,7},{6,8},{7,9},{8,10},{9,11},{10,... | collective-permute-start | bytes 393224 | tf_op jit(solution)/shard_map/ppermute | solution.py:13
  137.8 18.5 %collective-permute-start.7 = (bf16[2,256,128]{2,0,1:T(2,128)(2,1)S(1)}, bf16[2,256,128]{2,0,1:T(2,128)(2,1)S(1)}, u32[]{:S(2)}, u32[]{:S(2)}) collective-permute-start(bf16[2,256,128]{2,0,1:T(2,128)(2,1)S(1)} %copy.22), channel_id=1, source_target_pairs={{2,0},{3,1},{4,2},{5,3},{6,4},{7,5},{8,6},{9,7},{10,8},{11,9},{12,... | collective-permute-start | bytes 393224 | tf_op jit(solution)/shard_map/ppermute | solution.py:13
  146.4 42.3 %collective-permute-start.18 = (bf16[2,256,128]{2,0,1:T(2,128)(2,1)}, bf16[2,256,128]{2,0,1:T(2,128)(2,1)}, u32[]{:S(2)}, u32[]{:S(2)}) collective-permute-start(bf16[2,256,128]{2,0,1:T(2,128)(2,1)} %get-tuple-element.13), channel_id=1, source_target_pairs={{2,0},{3,1},{4,2},{5,3},{6,4},{7,5},{8,6},{9,7},{10,8},{11,9},{12,... | collective-permute-start | bytes 393224 | tf_op jit(solution)/shard_map/ppermute | solution.py:13
  148.3 41.7 %collective-permute-start.17 = (bf16[2,256,128]{2,0,1:T(2,128)(2,1)}, bf16[2,256,128]{2,0,1:T(2,128)(2,1)}, u32[]{:S(2)}, u32[]{:S(2)}) collective-permute-start(bf16[2,256,128]{2,0,1:T(2,128)(2,1)} %get-tuple-element.14), channel_id=1, source_target_pairs={{0,1},{1,2},{2,3},{3,4},{4,5},{5,6},{6,7},{7,8},{8,9},{9,10},{10,1... | collective-permute-start | bytes 393224 | tf_op jit(solution)/shard_map/ppermute | solution.py:13
  150.3 41.1 %collective-permute-start.16 = (bf16[2,256,128]{2,0,1:T(2,128)(2,1)}, bf16[2,256,128]{2,0,1:T(2,128)(2,1)}, u32[]{:S(2)}, u32[]{:S(2)}) collective-permute-start(bf16[2,256,128]{2,0,1:T(2,128)(2,1)} %get-tuple-element.11), channel_id=1, source_target_pairs={{1,0},{2,1},{3,2},{4,3},{5,4},{6,5},{7,6},{8,7},{9,8},{10,9},{11,1... | collective-permute-start | bytes 393224 | tf_op jit(solution)/shard_map/ppermute | solution.py:13
  205.7 21.4 %copy-start.9 = (f32[16,256,128]{2,0,1:T(8,128)}, f32[16,256,128]{2,0,1:T(8,128)S(1)}, u32[]{:S(2)}) copy-start(f32[16,256,128]{2,0,1:T(8,128)S(1)} %fusion) | copy-start | bytes 6291460
  205.7 20.1 %copy-start.7 = (bf16[8,256,128]{2,1,0:T(8,128)(2,1)S(1)}, bf16[8,256,128]{2,1,0:T(8,128)(2,1)}, u32[]{:S(2)}) copy-start(bf16[8,256,128]{2,1,0:T(8,128)(2,1)} %copy.25) | copy-start | bytes 1572868
  206.9 53.5 %collective-permute-start.22 = (bf16[2,256,128]{2,0,1:T(2,128)(2,1)}, bf16[2,256,128]{2,0,1:T(2,128)(2,1)}, u32[]{:S(2)}, u32[]{:S(2)}) collective-permute-start(bf16[2,256,128]{2,0,1:T(2,128)(2,1)} %get-tuple-element.9), channel_id=1, source_target_pairs={{2,0},{3,1},{4,2},{5,3},{6,4},{7,5},{8,6},{9,7},{10,8},{11,9},{12,... | collective-permute-start | bytes 393224 | tf_op jit(solution)/shard_map/ppermute | solution.py:13
  209.1 18.5 %collective-permute-start.10 = (bf16[2,256,128]{2,0,1:T(2,128)(2,1)S(1)}, bf16[2,256,128]{2,0,1:T(2,128)(2,1)S(1)}, u32[]{:S(2)}, u32[]{:S(2)}) collective-permute-start(bf16[2,256,128]{2,0,1:T(2,128)(2,1)S(1)} %copy.31), channel_id=1, source_target_pairs={{0,2},{1,3},{2,4},{3,5},{4,6},{5,7},{6,8},{7,9},{8,10},{9,11},{10,... | collective-permute-start | bytes 393224 | tf_op jit(solution)/shard_map/ppermute | solution.py:13
  214.7 14.8 %collective-permute-start.11 = (bf16[2,256,128]{2,0,1:T(2,128)(2,1)S(1)}, bf16[2,256,128]{2,0,1:T(2,128)(2,1)S(1)}, u32[]{:S(2)}, u32[]{:S(2)}) collective-permute-start(bf16[2,256,128]{2,0,1:T(2,128)(2,1)S(1)} %copy.33), channel_id=1, source_target_pairs={{2,0},{3,1},{4,2},{5,3},{6,4},{7,5},{8,6},{9,7},{10,8},{11,9},{12,... | collective-permute-start | bytes 393224 | tf_op jit(solution)/shard_map/ppermute | solution.py:13
  217.8 16.5 %collective-permute-start.8 = (bf16[2,256,128]{2,0,1:T(2,128)(2,1)S(1)}, bf16[2,256,128]{2,0,1:T(2,128)(2,1)S(1)}, u32[]{:S(2)}, u32[]{:S(2)}) collective-permute-start(bf16[2,256,128]{2,0,1:T(2,128)(2,1)S(1)} %copy.27), channel_id=1, source_target_pairs={{0,1},{1,2},{2,3},{3,4},{4,5},{5,6},{6,7},{7,8},{8,9},{9,10},{10,1... | collective-permute-start | bytes 393224 | tf_op jit(solution)/shard_map/ppermute | solution.py:13
  220.7 17.1 %collective-permute-start.9 = (bf16[2,256,128]{2,0,1:T(2,128)(2,1)S(1)}, bf16[2,256,128]{2,0,1:T(2,128)(2,1)}, u32[]{:S(2)}, u32[]{:S(2)}) collective-permute-start(bf16[2,256,128]{2,0,1:T(2,128)(2,1)S(1)} %copy.29), channel_id=1, source_target_pairs={{1,0},{2,1},{3,2},{4,3},{5,4},{6,5},{7,6},{8,7},{9,8},{10,9},{11,1... | collective-permute-start | bytes 393224 | tf_op jit(solution)/shard_map/ppermute | solution.py:13
  227.6 35.1 %collective-permute-start.21 = (bf16[2,256,128]{2,0,1:T(2,128)(2,1)}, bf16[2,256,128]{2,0,1:T(2,128)(2,1)}, u32[]{:S(2)}, u32[]{:S(2)}) collective-permute-start(bf16[2,256,128]{2,0,1:T(2,128)(2,1)} %get-tuple-element.10), channel_id=1, source_target_pairs={{0,1},{1,2},{2,3},{3,4},{4,5},{5,6},{6,7},{7,8},{8,9},{9,10},{10,1... | collective-permute-start | bytes 393224 | tf_op jit(solution)/shard_map/ppermute | solution.py:13
  229.5 35.4 %collective-permute-start.23 = (bf16[2,256,128]{2,0,1:T(2,128)(2,1)}, bf16[2,256,128]{2,0,1:T(2,128)(2,1)}, u32[]{:S(2)}, u32[]{:S(2)}) collective-permute-start(bf16[2,256,128]{2,0,1:T(2,128)(2,1)} %get-tuple-element.8), channel_id=1, source_target_pairs={{0,2},{1,3},{2,4},{3,5},{4,6},{5,7},{6,8},{7,9},{8,10},{9,11},{10,... | collective-permute-start | bytes 393224 | tf_op jit(solution)/shard_map/ppermute | solution.py:13
  234.3 79.2 %collective-permute-start.20 = (bf16[2,256,128]{2,0,1:T(2,128)(2,1)}, bf16[2,256,128]{2,0,1:T(2,128)(2,1)S(1)}, u32[]{:S(2)}, u32[]{:S(2)}) collective-permute-start(bf16[2,256,128]{2,0,1:T(2,128)(2,1)} %get-tuple-element.7), channel_id=1, source_target_pairs={{1,0},{2,1},{3,2},{4,3},{5,4},{6,5},{7,6},{8,7},{9,8},{10,9},{11,1... | collective-permute-start | bytes 393224 | tf_op jit(solution)/shard_map/ppermute | solution.py:13
  260.3 273.6 %all-reduce.5.cloned.1.call-start = ((), (), s32[]{:S(2)}) async-start(), calls=%async_computation.1 | async-start | bytes 524288 | tf_op jit(solution)/shard_map/psum | solution.py:115
  (37 other events, 193.9 us)
Sparse Core Ops, SparseCore 0:
  260.4 52.9 all-reduce.2
  319.7 214.0 all-reduce.4
